TPU v7x, 256 devices: a whole 4x4x8 slice. The times are simulated.
256 devices in a mesh: blk: 128 (over x, z, y), row: 2 (over core).
Axes of the slice: x: 4, y: 4, z: 8, core: 2. Of those that a mesh axis runs over, the one named last changes fastest.
Arguments:
- diag_block: float32 [1024, 1024], P('row'), as said below
- panel_rows: float32 [2, 4096, 1024], P('row', 'blk'), may hold values from -6 to 6
- row_ids: int32 [32], replicated, may hold values from 0 to 255, as said below
- col_ids: int32 [768], P('blk'), may hold values from -1 to 255, as said below
- block_rows: int32 [768, 8], P('blk'), may hold values from -1 to 255, as said below
- blocks: float32 [768, 8, 256, 256], P('blk', None, 'row'), may hold values from -6 to 6
Outputs:
- factor_rows: float32 [2, 4096, 1024], P('row', 'blk')
- new_blocks: float32 [768, 8, 256, 256], P('blk', None, 'row')
Inputs may be any that keep to these rules, and one draw needn't show every extreme that they name: `row_ids`: strictly increasing and distinct; the last is 255. `col_ids`: each of the 256 block columns stands in exactly one slot; an owner's slots s * 6 to s * 6 + 5 hold its columns first, then -1; owners hold 0 to 6 columns, one owner exactly 6. `block_rows`: for a live slot, entry 0 is its own column, live entries rise strictly and are followed only by -1; an empty slot holds -1 only. A column among row_ids stores the block rows of row_ids from itself on, up to 8 of them. `diag_block`: symmetric positive definite.
All inputs are finite; a program needn't handle non-finite values.
Results may differ from a plain program's by a relative error of at most 0.0003.
Values may be sent and summed in bfloat16 or wider, within the bound.
A program may use at most 128 MiB of HBM per device.

v0:
```python
import jax
import jax.numpy as jnp
from jax import lax
from jax.sharding import PartitionSpec as P


def right_solve(lower_factor, right_side):
    return lax.linalg.triangular_solve(
        lower_factor, right_side, left_side=False, lower=True, transpose_a=True
    )


def local(diag_block, panel_rows, row_ids, col_ids, block_rows, blocks):
    diag_full = lax.all_gather(diag_block, "row", axis=0, tiled=True)
    panel_width = diag_full.shape[0] // 2
    diag_first = diag_full[:panel_width, :panel_width]
    coupling = diag_full[panel_width:, :panel_width]
    diag_second = diag_full[panel_width:, panel_width:]
    factor_first = jnp.linalg.cholesky(diag_first)
    own_rows = panel_rows[0]
    left_part = right_solve(factor_first, own_rows[:, :panel_width])
    coupled = right_solve(factor_first, coupling)
    schur_second = diag_second - jnp.dot(coupled, coupled.T, precision=lax.Precision.HIGHEST)
    factor_second = jnp.linalg.cholesky(schur_second)
    right_rows = own_rows[:, panel_width:] - jnp.dot(
        left_part, coupled.T, precision=lax.Precision.HIGHEST
    )
    right_part = right_solve(factor_second, right_rows)
    factor = jnp.concatenate([left_part, right_part], axis=1)
    rounded = factor.astype(jnp.bfloat16)[None]
    pieces = row_ids.shape[0]
    half_rows = blocks.shape[2]
    pick_col = ((row_ids[None, :] == col_ids[:, None]) & (col_ids[:, None] >= 0)).astype(
        jnp.bfloat16
    )
    pick_rows = (
        (row_ids[None, None, :] == block_rows[:, :, None]) & (block_rows[:, :, None] >= 0)
    ).astype(jnp.bfloat16)
    core_index = lax.axis_index("row")
    gathered = lax.all_gather(rounded[None], ("blk", "row"), axis=0, tiled=True)
    layered = gathered.reshape(-1, 2, gathered.shape[2], gathered.shape[3])
    by_block = layered.transpose(1, 0, 2, 3).reshape(2, pieces, half_rows, 2 * panel_width)
    my_half = lax.dynamic_index_in_dim(by_block, core_index, 0, keepdims=False)
    col_parts = jnp.einsum("sk,hkab->shab", pick_col, by_block, preferred_element_type=jnp.float32)
    col_factor = col_parts.astype(jnp.bfloat16).reshape(
        col_ids.shape[0], 2 * half_rows, 2 * panel_width
    )
    row_factor = jnp.einsum(
        "srk,kab->srab", pick_rows, my_half, preferred_element_type=jnp.float32
    ).astype(jnp.bfloat16)
    change = jnp.einsum(
        "srab,sjb->sraj", row_factor, col_factor, preferred_element_type=jnp.float32
    )
    return (factor[None], blocks - change)


def solution(mesh):
    return jax.shard_map(
        local,
        mesh=mesh,
        in_specs=(
            P("row", None),
            P("row", "blk", None),
            P(),
            P("blk"),
            P("blk", None),
            P("blk", None, "row", None),
        ),
        out_specs=(P("row", "blk", None), P("blk", None, "row", None)),
        check_vma=False,
    )
```

profile of v0, /device:TPU:1, one launch (start us, length us, event | category | flops | bytes accessed | tf_op | source)
XLA Modules:
  0.0 543.3 jit_solution(3519168554521171538)
XLA Ops:
  7.2 2.9 copy.31
  10.2 23.8 %all-gather.3.cloned.1.call-done = f32[1024,1024]{0,1:T(8,128)} async-done(((f32[512,1024]{0,1:T(8,128)}), f32[1024,1024]{0,1:T(8,128)}) %all-gather.3.cloned.1.call-update) | async-done | bytes 4194320 | tf_op jit(solution)/shard_map/all_gather | solution.py:14
  35.6 1.5 fusion.20
  37.1 11.7 %cholesky.286 = f32[128,128]{1,0:T(8,128)S(1)} custom-call(f32[128,128]{1,0:T(8,128)S(1)} %cholesky.426), custom_call_target="Cholesky" | custom-call | tf_op jit(solution)/shard_map/jit(cholesky)/cholesky | solution.py:19
  49.0 9.8 %custom-call.31 = f32[1,128,128]{1,2,0:T(8,128)S(1)} custom-call(f32[1,128,128]{2,1,0:T(8,128)S(1)} %get-tuple-element.67), custom_call_target="InvertDiagBlocksLowerTriangular" | custom-call | tf_op jit(solution)/shard_map/jit(cholesky)/cholesky | solution.py:19
  59.5 11.7 %cholesky.305 = f32[128,128]{1,0:T(8,128)S(1)} custom-call(f32[128,128]{1,0:T(8,128)S(1)} %cholesky.430), custom_call_target="Cholesky" | custom-call | tf_op jit(solution)/shard_map/jit(cholesky)/cholesky | solution.py:19
  71.2 10.2 %custom-call.32 = f32[1,128,128]{1,2,0:T(8,128)S(1)} custom-call(f32[1,128,128]{2,1,0:T(8,128)S(1)} %get-tuple-element.64), custom_call_target="InvertDiagBlocksLowerTriangular" | custom-call | tf_op jit(solution)/shard_map/jit(cholesky)/cholesky | solution.py:19
  82.1 11.7 %cholesky.326 = f32[128,128]{1,0:T(8,128)S(1)} custom-call(f32[128,128]{1,0:T(8,128)S(1)} %cholesky.435), custom_call_target="Cholesky" | custom-call | tf_op jit(solution)/shard_map/jit(cholesky)/cholesky | solution.py:19
  93.9 9.8 %custom-call.33 = f32[1,128,128]{1,2,0:T(8,128)S(1)} custom-call(f32[1,128,128]{2,1,0:T(8,128)S(1)} %get-tuple-element.61), custom_call_target="InvertDiagBlocksLowerTriangular" | custom-call | tf_op jit(solution)/shard_map/jit(cholesky)/cholesky | solution.py:19
  104.3 11.7 %cholesky.343 = f32[128,128]{1,0:T(8,128)S(1)} custom-call(f32[128,128]{1,0:T(8,128)S(1)} %convolution_subtract_fusion.10), custom_call_target="Cholesky" | custom-call | tf_op jit(solution)/shard_map/jit(cholesky)/cholesky | solution.py:19
  120.9 8.0 %while.5 = (s32[]{:T(128)}, f32[512,512]{1,0:T(8,128)S(1)}, s32[4,2]{0,1:T(2,128)S(1)}, f32[4,128,128]{2,1,0:T(8,128)S(1)}, s32[]{:T(128)}) while((s32[]{:T(128)}, f32[512,512]{1,0:T(8,128)S(1)}, s32[4,2]{0,1:T(2,128)S(1)}, f32[4,128,128]{2,1,0:T(8,128)S(1)}, s32[]{:T(128)}) %tuple.58), condition=%wide.while_cond, body=%wide.while_body.sunk | while | flops 2 | bytes 131189 | solution.py:8
  128.9 39.3 %custom-call.34 = f32[4,128,128]{1,2,0:T(8,128)S(1)} custom-call(f32[4,128,128]{2,1,0:T(8,128)S(1)} %get-tuple-element.26), custom_call_target="InvertDiagBlocksLowerTriangular" | custom-call | tf_op jit(solution)/shard_map/triangular_solve/custom-call.3 | solution.py:8
  173.2 1.6 convolution_subtract_fusion.3
  177.5 3.2 convolution_subtract_fusion
  181.2 11.7 %cholesky.358 = f32[128,128]{1,0:T(8,128)S(1)} custom-call(f32[128,128]{1,0:T(8,128)S(1)} %cholesky.439), custom_call_target="Cholesky" | custom-call | tf_op jit(solution)/shard_map/jit(cholesky)/cholesky | solution.py:24
  193.1 10.0 %custom-call.35 = f32[1,128,128]{1,2,0:T(8,128)S(1)} custom-call(f32[1,128,128]{2,1,0:T(8,128)S(1)} %get-tuple-element.57), custom_call_target="InvertDiagBlocksLowerTriangular" | custom-call | tf_op jit(solution)/shard_map/jit(cholesky)/cholesky | solution.py:24
  203.8 11.7 %cholesky.377 = f32[128,128]{1,0:T(8,128)S(1)} custom-call(f32[128,128]{1,0:T(8,128)S(1)} %cholesky.443), custom_call_target="Cholesky" | custom-call | tf_op jit(solution)/shard_map/jit(cholesky)/cholesky | solution.py:24
  215.5 9.8 %custom-call.36 = f32[1,128,128]{1,2,0:T(8,128)S(1)} custom-call(f32[1,128,128]{2,1,0:T(8,128)S(1)} %get-tuple-element.54), custom_call_target="InvertDiagBlocksLowerTriangular" | custom-call | tf_op jit(solution)/shard_map/jit(cholesky)/cholesky | solution.py:24
  226.0 11.7 %cholesky.398 = f32[128,128]{1,0:T(8,128)S(1)} custom-call(f32[128,128]{1,0:T(8,128)S(1)} %cholesky.448), custom_call_target="Cholesky" | custom-call | tf_op jit(solution)/shard_map/jit(cholesky)/cholesky | solution.py:24
  237.7 10.2 %custom-call.37 = f32[1,128,128]{1,2,0:T(8,128)S(1)} custom-call(f32[1,128,128]{2,1,0:T(8,128)S(1)} %get-tuple-element.51), custom_call_target="InvertDiagBlocksLowerTriangular" | custom-call | tf_op jit(solution)/shard_map/jit(cholesky)/cholesky | solution.py:24
  248.5 11.7 %cholesky.415 = f32[128,128]{1,0:T(8,128)S(1)} custom-call(f32[128,128]{1,0:T(8,128)S(1)} %convolution_subtract_fusion.9), custom_call_target="Cholesky" | custom-call | tf_op jit(solution)/shard_map/jit(cholesky)/cholesky | solution.py:24
  265.6 8.5 %while.6 = (s32[]{:T(128)}, f32[512,512]{1,0:T(8,128)S(1)}, s32[4,2]{0,1:T(2,128)S(1)}, f32[4,128,128]{2,1,0:T(8,128)S(1)}, s32[]{:T(128)}) while((s32[]{:T(128)}, f32[512,512]{1,0:T(8,128)S(1)}, s32[4,2]{0,1:T(2,128)S(1)}, f32[4,128,128]{2,1,0:T(8,128)S(1)}, s32[]{:T(128)}) %tuple.68), condition=%wide.while_cond.clone, body=%wide.while_body.clone.sunk | while | flops 2 | bytes 131189 | solution.py:8
  266.3 1.4 bitcast_dynamic-update-slice_fusion.5
  268.4 1.4 bitcast_dynamic-update-slice_fusion.5
  270.6 1.4 bitcast_dynamic-update-slice_fusion.5
  274.1 39.3 %custom-call.38 = f32[4,128,128]{1,2,0:T(8,128)S(1)} custom-call(f32[4,128,128]{2,1,0:T(8,128)S(1)} %get-tuple-element.27), custom_call_target="InvertDiagBlocksLowerTriangular" | custom-call | tf_op jit(solution)/shard_map/triangular_solve/custom-call.3 | solution.py:8
  316.3 125.3 %all-gather.5.cloned.1.call-done = bf16[256,1,32,1024]{3,2,1,0:T(8,128)(2,1)} async-done(((bf16[1,1,32,1024]{3,2,1,0:T(8,128)(2,1)}), bf16[256,1,32,1024]{3,2,1,0:T(8,128)(2,1)}) %all-gather.5.cloned.1.call-update) | async-done | bytes 16777232 | tf_op jit(solution)/shard_map/all_gather | solution.py:40
  441.6 14.4 %copy.38 = bf16[2,128,32,1024]{3,2,1,0:T(8,128)(2,1)} copy(bf16[2,128,32,1024]{3,2,0,1:T(8,128)(2,1)} %bitcast.146) | data formatting | bytes 33554432 | tf_op jit(solution)/shard_map/transpose | solution.py:42
  456.0 8.2 %constant_dynamic-slice_fusion.2 = bf16[1,32,128,1024]{3,2,1,0:T(8,128)(2,1)} fusion(bf16[2,32,128,1024]{3,2,1,0:T(8,128)(2,1)} %bitcast.144, s32[]{:T(128)S(6)} %select_n.7), kind=kLoop, calls=%fused_computation.174 | loop fusion | bytes 16777220 | tf_op jit(solution)/shard_map/jit(dynamic_index_in_dim)/dynamic_slice | solution.py:43
  464.2 25.7 %fusion.11 = bf16[6,2,128,1024]{3,0,2,1:T(8,128)(2,1)} fusion(bf16[2,32,128,1024]{3,2,1,0:T(8,128)(2,1)} %bitcast.145, s32[32]{0:T(128)S(1)} %copy-done.2, s32[6]{0:T(128)S(1)} %copy-done.3, pred[6]{0:T(512)(128)(4,1)S(1)} %broadcast_compare_fusion.1), kind=kOutput, calls=%fused_computation.13 | convolution fusion | flops 102236544 | bytes 19923102 | tf_op jit(solution)/shard_map/sk,hkab->shab/dot_general | solution.py:44
  489.9 20.6 %fusion.7 = bf16[6,8,128,1024]{3,1,2,0:T(8,128)(2,1)} fusion(bf16[1,32,128,1024]{3,2,1,0:T(8,128)(2,1)} %constant_dynamic-slice_fusion.2, s32[6,8]{1,0:T(8,128)S(1)} %copy-done, s32[32]{0:T(128)S(1)} %copy-done.2, pred[6,8]{1,0:T(8,128)(4,1)S(1)} %broadcast_compare_fusion), kind=kOutput, calls=%fused_computation.11 | convolution fusion | flops 408947712 | bytes 20971888 | tf_op jit(solution)/shard_map/srk,kab->srab/dot_general | solution.py:48
  510.6 25.6 %fusion.14 = f32[6,8,128,256]{3,2,1,0:T(8,128)} fusion(f32[6,8,128,256]{3,2,1,0:T(8,128)} %param.14, bf16[6,256,1024,1]{2,0,1,3:T(8,128)(2,1)} %bitcast.151, bf16[6,8,128,1024]{3,1,2,0:T(8,128)(2,1)} %fusion.7), kind=kOutput, calls=%fused_computation.14 | convolution fusion | flops 3222798336 | bytes 28311552 | tf_op jit(solution)/shard_map/srab,sjb->sraj/dot_general | solution.py:51
  (105 shorter events, 34.0 us)
Async XLA Ops:
  7.2 26.8 %all-gather.3.cloned.1.call-start = ((), (), s32[]{:S(2)}) async-start(), calls=%async_computation | async-start | bytes 6291456 | tf_op jit(solution)/shard_map/all_gather | solution.py:14
  10.1 431.5 %all-gather.5.cloned.1.call-start = ((), (), s32[]{:S(2)}) async-start(), calls=%async_computation.1 | async-start | bytes 16842752 | tf_op jit(solution)/shard_map/all_gather | solution.py:40
  35.6 139.6 %copy-start.1 = (f32[1,32,1024]{2,1,0:T(8,128)S(1)}, f32[1,32,1024]{2,1,0:T(8,128)}, u32[]{:S(2)}) copy-start(f32[1,32,1024]{2,1,0:T(8,128)} %param.10) | copy-start | bytes 393220
  177.4 138.2 %copy-start.3 = (s32[6]{0:T(128)S(1)}, s32[6]{0:T(128)}, u32[]{:S(2)}) copy-start(s32[6]{0:T(128)} %param.12) | copy-start | bytes 76
  177.5 138.2 %copy-start = (s32[6,8]{1,0:T(8,128)S(1)}, s32[6,8]{1,0:T(8,128)}, u32[]{:S(2)}) copy-start(s32[6,8]{1,0:T(8,128)} %param.13) | copy-start | bytes 580
  456.0 8.2 %copy-start.2 = (s32[32]{0:T(128)S(1)}, s32[32]{0:T(128)}, u32[]{:S(2)}) copy-start(s32[32]{0:T(128)} %param.11) | copy-start | bytes 388
Sparse Core Ops, SparseCore 0:
  10.4 23.5 all-gather.2
  315.7 125.8 all-gather.4
where the time goes:
time: 553 us; the launch traced here: 543 us
  other arithmetic  241 us (44%)
  waiting for transfers between devices  149 us (27%)
  matrix products  89.4 us (16%)
  local copies, waits for them, and re-layouts  44 us (8%)
  between operations  19.8 us (4%)
    all_gather x1, waiting for transfers between devices, local(): gathered = lax.all_gather(rounded[None], ('blk', 'row'), axis=0, tiled=True)  125 us
    another operation x15, other arithmetic, local(): factor_second = jnp.linalg.cholesky(schur_second)  79.6 us
    another operation x5, other arithmetic, right_solve(): lax.linalg.triangular_solve(lower_factor, right_side, left_side=False, lo...  79.1 us
    another operation x14, other arithmetic, local(): factor_first = jnp.linalg.cholesky(diag_first)  78.9 us
    dot_general x1, matrix products, local(): jnp.einsum('sk,hkab->shab', pick_col, by_block, preferred_element_type=jn...  25.7 us
    dot_general x1, matrix products, local(): jnp.einsum('srab,sjb->sraj', row_factor, col_factor, preferred_element_ty...  25.6 us
    all_gather x1, waiting for transfers between devices, local(): diag_full = lax.all_gather(diag_block, 'row', axis=0, tiled=True)  23.8 us
    dot_general x1, matrix products, local(): jnp.einsum('srk,kab->srab', pick_rows, my_half, preferred_element_type=jn...  20.6 us
  transfers between devices with their start and end apart: 2, of which 2 were waited for; matrix products, arithmetic and copies ran while one was open for 0% of the time, Pallas kernels for 0%

commit v1 on v0

v1 whole, which is shorter than its diff:
```python
import functools

import jax
import jax.numpy as jnp
from jax import lax
from jax.experimental import pallas as pl
from jax.experimental.pallas import tpu as pltpu
from jax.sharding import PartitionSpec as P

HIGH = lax.Precision.HIGHEST
NB = 128
F32 = jnp.float32


def lane_spread(x, c):
    return jnp.broadcast_to(x[:, c : c + 1], x.shape)


def row_spread(x, m):
    return jnp.broadcast_to(x[m : m + 1, :], x.shape)


def reciprocal(d):
    r = pl.reciprocal(d, approx=True)
    return r * (2.0 - d * r)


def mm(a, b, ca, cb):
    return lax.dot_general(
        a, b, (((ca,), (cb,)), ((), ())), precision=HIGH, preferred_element_type=F32
    )


def block_inverse(rows):
    sub = lax.broadcasted_iota(jnp.int32, (8, NB), 0)
    lane = lax.broadcasted_iota(jnp.int32, (8, NB), 1)
    n = NB // 8
    a = list(rows)
    e = [jnp.where(lane == sub + 8 * k, 1.0, 0.0).astype(F32) for k in range(n)]
    inverse = [None] * n
    pivot = [lane_spread(a[0], m) for m in range(8)]
    for j in range(n):
        d = list(pivot)
        unit = [jnp.where(sub == m, 1.0, 0.0).astype(F32) for m in range(8)]
        diagonal = jnp.ones((8, NB), F32)
        for i in range(8):
            top = row_spread(d[i], i)
            diagonal = jnp.where(sub == i, top, diagonal)
            if i == 7:
                break
            f = jnp.where(sub > i, d[i] * reciprocal(top), 0.0)
            for m in range(i + 1, 8):
                d[m] = d[m] - f * row_spread(d[i], m)
            for m in range(i + 1):
                unit[m] = unit[m] - f * row_spread(unit[m], i)
        scale = lax.rsqrt(diagonal)
        scale = scale * (1.5 - 0.5 * diagonal * scale * scale)
        w = [unit[m] * scale for m in range(8)]
        u = w[0] * row_spread(a[j], 0)
        v = w[0] * row_spread(e[j], 0)
        for m in range(1, 8):
            u = u + w[m] * row_spread(a[j], m)
            v = v + w[m] * row_spread(e[j], m)
        inverse[j] = v
        if j == n - 1:
            break
        ws = {(i, m): row_spread(w[m], i) for i in range(8) for m in range(i + 1)}
        us = [row_spread(u, i) for i in range(8)]
        vs = [row_spread(v, i) for i in range(8)]
        for k in range(j + 1, n):
            below = [lane_spread(a[k], 8 * j + m) for m in range(8)]
            c = []
            for i in range(8):
                t = below[0] * ws[i, 0]
                for m in range(1, i + 1):
                    t = t + below[m] * ws[i, m]
                c.append(t)
            if k == j + 1:
                pivot = []
                for m in range(8):
                    t = c[0] * row_spread(c[0], m)
                    for i in range(1, 8):
                        t = t + c[i] * row_spread(c[i], m)
                    pivot.append(lane_spread(a[k], 8 * k + m) - t)
            ta, te = c[0] * us[0], c[0] * vs[0]
            for i in range(1, 8):
                ta = ta + c[i] * us[i]
                te = te + c[i] * vs[i]
            a[k] = a[k] - ta
            e[k] = e[k] - te
    return jnp.concatenate(inverse, axis=0)


def factor_kernel(s_ref, r_ref, blocks_ref, x_ref, g_ref, copy_ref, u_ref, t_ref, linv_ref, dg_ref, y_ref, sem):
    steps = s_ref.shape[0] // NB
    copy = pltpu.make_async_copy(blocks_ref, copy_ref, sem)
    copy.start()
    u_ref[...] = jnp.zeros_like(u_ref)
    x_ref[...] = jnp.zeros_like(x_ref)
    linv_ref[...] = jnp.zeros_like(linv_ref)
    t_ref[1] = jnp.zeros(t_ref.shape[1:], F32)
    t_ref[0] = s_ref[0:NB, :]
    dg_ref[...] = s_ref[0:NB, 0:NB]
    y_ref[...] = r_ref[:, 0:NB]

    def step(p, carry):
        cur = lax.rem(p, 2)
        oth = 1 - cur
        here = pl.ds(pl.multiple_of(p * NB, NB), NB)
        before = pl.ds(pl.multiple_of(jnp.maximum(p - 1, 0) * NB, NB), NB)
        after = pl.ds(pl.multiple_of(jnp.minimum(p + 1, steps - 1) * NB, NB), NB)
        u_prev = mm(linv_ref[...], t_ref[oth], 1, 0)
        u_ref[before, :] = u_prev
        t_ref[cur] = t_ref[cur] - mm(u_ref[before, here], u_prev, 0, 0)
        t_next = s_ref[after, :] - mm(u_ref[:, after], u_ref[...], 0, 0)
        y_next = r_ref[:, after] - mm(x_ref[...], u_ref[:, after], 1, 0)
        linv = block_inverse([dg_ref[8 * k : 8 * k + 8, :] for k in range(NB // 8)])
        linv_ref[...] = linv
        t_ref[oth] = t_next
        u_after = mm(linv, t_ref[cur, :, after], 1, 0)
        dg_ref[...] = t_ref[oth, :, after] - mm(u_after, u_after, 0, 0)
        x_here = mm(y_ref[...], linv, 1, 1)
        x_ref[:, here] = x_here
        g_ref[p] = x_here.astype(jnp.bfloat16)
        y_ref[...] = y_next - mm(x_here, u_after, 1, 0)
        return carry

    lax.fori_loop(0, steps, step, 0)
    copy.wait()


def factor(diag, rows, blocks):
    order = diag.shape[0]
    vmem = pl.BlockSpec(memory_space=pltpu.VMEM)
    anywhere = pl.BlockSpec(memory_space=pl.ANY)
    return pl.pallas_call(
        factor_kernel,
        out_shape=(
            jax.ShapeDtypeStruct(rows.shape, F32),
            jax.ShapeDtypeStruct((order // NB, rows.shape[0], NB), jnp.bfloat16),
            jax.ShapeDtypeStruct(blocks.shape, F32),
        ),
        in_specs=[vmem, vmem, anywhere],
        out_specs=[vmem, vmem, anywhere],
        scratch_shapes=[
            pltpu.VMEM((order, order), F32),
            pltpu.VMEM((2, NB, order), F32),
            pltpu.VMEM((NB, NB), F32),
            pltpu.VMEM((NB, NB), F32),
            pltpu.VMEM((rows.shape[0], NB), F32),
            pltpu.SemaphoreType.DMA,
        ],
        compiler_params=pltpu.CompilerParams(vmem_limit_bytes=48 << 20),
    )(diag, rows, blocks)


def update_kernel(col_at, row_at, half, g_ref, blocks_ref, out_ref, col_buf, row_buf, blk_buf, col_sem, row_sem, blk_sem):
    slots, stored = blocks_ref.shape[:2]
    chunks = g_ref.shape[0]
    size = blk_buf.shape[2]
    mine = half[0]
    last = g_ref.shape[2] - 1

    def col_copy(s):
        return pltpu.make_async_copy(g_ref.at[:, :, jnp.maximum(col_at[s], 0)], col_buf.at[s], col_sem.at[s])

    def row_copy(s, r):
        at = jnp.minimum(jnp.maximum(row_at[s, r], 0), last)
        return pltpu.make_async_copy(g_ref.at[:, mine, at], row_buf.at[s, r], row_sem.at[s, r])

    def blk_in(s):
        return pltpu.make_async_copy(blocks_ref.at[s], blk_buf.at[s], blk_sem.at[s])

    def blk_out(s):
        return pltpu.make_async_copy(blk_buf.at[s], out_ref.at[s], blk_sem.at[s])

    for s in range(slots):
        @pl.when(col_at[s] >= 0)
        def _():
            col_copy(s).start()
            for r in range(stored):
                row_copy(s, r).start()
            blk_in(s).start()

    for s in range(slots):
        @pl.when(col_at[s] >= 0)
        def _():
            col_copy(s).wait()
            for r in range(stored):
                row_copy(s, r).wait()
            blk_in(s).wait()

            @pl.loop(0, stored)
            def _(r):
                total = jnp.zeros((size, 2 * size), F32)
                for p in range(0, chunks, 2):
                    left = [row_buf[s, r, p + q].reshape(size, NB) for q in range(2)]
                    right = [col_buf[s, p + q].reshape(2 * size, NB) for q in range(2)]
                    total += lax.dot_general(
                        jnp.concatenate(left, axis=1),
                        jnp.concatenate(right, axis=1),
                        (((1,), (1,)), ((), ())),
                        preferred_element_type=F32,
                    )
                kept = blk_buf[s, r]
                blk_buf[s, r] = jnp.where(row_at[s, r] >= 0, kept - total, kept)

            blk_out(s).start()

    for s in range(slots):
        @pl.when(col_at[s] >= 0)
        def _():
            blk_out(s).wait()


def update(g, blocks, col_at, row_at, half):
    slots, stored, size, width = blocks.shape
    chunks, _, _, parts, rows, _ = g.shape
    smem = pl.BlockSpec(memory_space=pltpu.SMEM)
    anywhere = pl.BlockSpec(memory_space=pl.ANY)
    return pl.pallas_call(
        update_kernel,
        out_shape=jax.ShapeDtypeStruct(blocks.shape, F32),
        in_specs=[smem, smem, smem, anywhere, anywhere],
        out_specs=anywhere,
        scratch_shapes=[
            pltpu.VMEM((slots, chunks, 2, parts, rows, NB), jnp.bfloat16),
            pltpu.VMEM((slots, stored, chunks, parts, rows, NB), jnp.bfloat16),
            pltpu.VMEM((slots, stored, size, width), F32),
            pltpu.SemaphoreType.DMA((slots,)),
            pltpu.SemaphoreType.DMA((slots, stored)),
            pltpu.SemaphoreType.DMA((slots,)),
        ],
        input_output_aliases={4: 0},
        compiler_params=pltpu.CompilerParams(vmem_limit_bytes=40 << 20),
    )(col_at, row_at, half, g, blocks)


def places(ids, row_ids):
    match = (row_ids == ids[..., None]) & (ids[..., None] >= 0)
    at = jnp.arange(row_ids.shape[0], dtype=jnp.int32)
    return jnp.max(jnp.where(match, at, -1), axis=-1)


def local(diag_block, panel_rows, row_ids, col_ids, block_rows, blocks):
    pieces = row_ids.shape[0]
    diag = lax.all_gather(diag_block, "row", axis=0, tiled=True)
    x, g, kept = factor(diag, panel_rows[0], blocks)
    gathered = lax.all_gather(g, ("blk", "row"), axis=0, tiled=False)
    chunks, rows = g.shape[:2]
    gathered = gathered.reshape(pieces, -1, 2, chunks, rows, NB).transpose(3, 2, 0, 1, 4, 5)
    col_at = places(col_ids, row_ids)
    row_at = places(block_rows, row_ids)
    half = lax.axis_index("row").astype(jnp.int32)[None]
    return x[None], update(gathered, kept, col_at, row_at, half)


def solution(mesh):
    return jax.shard_map(
        local,
        mesh=mesh,
        in_specs=(
            P("row", None),
            P("row", "blk", None),
            P(),
            P("blk"),
            P("blk", None),
            P("blk", None, "row", None),
        ),
        out_specs=(P("row", "blk", None), P("blk", None, "row", None)),
        check_vma=False,
    )
```

time: 553 us -> 387 us (0.70); the launches traced: 543 us -> 387 us
  other arithmetic: 241 us -> 0.45 us
  Pallas kernels: 0 us -> 202 us
  matrix products: 89.4 us -> 0 us
  local copies, waits for them, and re-layouts: 44 us -> 18.7 us
  between operations: 19.8 us -> 14.1 us
    another operation x34 -> x0, other arithmetic: 238 us -> none  [the longest x15 79.6 us: local(): factor_second = jnp.linalg.cholesky(schur_second)]
    pallas_call x0 -> x2, Pallas kernels: none -> 202 us  [the longest x1 192 us: factor(): pl.pallas_call(factor_kernel, out_shape=(jax.ShapeDtypeStruct(rows.shape,...]
    dot_general x5 -> x0, matrix products: 75.9 us -> none  [the longest x1 25.7 us: local(): jnp.einsum('sk,hkab->shab', pick_col, by_block, preferred_element_type=jn...]
    another operation x35 -> x0, local copies, waits for them, and re-layouts: 16.6 us -> none  [the longest x27 16.3 us: right_solve(): lax.linalg.triangular_solve(lower_factor, right_side, left_side=False, lo...]
    reshape x0 -> x1, local copies, waits for them, and re-layouts: none -> 15.6 us  [local(): gathered.reshape(pieces, -1, 2, chunks, rows, NB)]
    transpose x1 -> x0, local copies, waits for them, and re-layouts: 14.4 us -> none  [local(): layered.transpose(1, 0, 2, 3).reshape(2, pieces, half_rows, 2 * panel_width)]
    another operation x33 -> x0, matrix products: 13.6 us -> none  [the longest x21 9.84 us: right_solve(): lax.linalg.triangular_solve(lower_factor, right_side, left_side=False, lo...]
    dynamic_slice x1 -> x0, local copies, waits for them, and re-layouts: 8.2 us -> none  [local(): my_half = lax.dynamic_index_in_dim(by_block, core_index, 0, keepdims=False)]
where the time goes in v1:
time: 387 us
  Pallas kernels  202 us (52%)
  waiting for transfers between devices  152 us (39%)
  local copies, waits for them, and re-layouts  18.7 us (5%)
  between operations  14.1 us (4%)
    pallas_call x1, Pallas kernels, factor(): pl.pallas_call(factor_kernel, out_shape=(jax.ShapeDtypeStruct(rows.shape,...  192 us
    all_gather x1, waiting for transfers between devices, local(): gathered = lax.all_gather(g, ('blk', 'row'), axis=0, tiled=False)  126 us
    all_gather x1, waiting for transfers between devices, local(): diag = lax.all_gather(diag_block, 'row', axis=0, tiled=True)  25.4 us
    reshape x1, local copies, waits for them, and re-layouts, local(): gathered.reshape(pieces, -1, 2, chunks, rows, NB)  15.6 us
    pallas_call x1, Pallas kernels, update(): pl.pallas_call(update_kernel, out_shape=jax.ShapeDtypeStruct(blocks.shape...  9.78 us
  transfers between devices with their start and end apart: 2, of which 2 were waited for; matrix products, arithmetic and copies ran while one was open for 0% of the time, Pallas kernels for 0%

profile of v1, /device:TPU:1, one launch (start us, length us, event | category | flops | bytes accessed | tf_op | source)
XLA Modules:
  0.0 387.2 jit_solution(16019351399294599080)
XLA Ops:
  7.2 0.0 copy-start.4
  7.2 0.0 copy-start.3
  7.2 0.0 copy-start.2
  7.2 0.0 all-gather.4.cloned.1.call-start
  7.2 0.7 all-gather.4.cloned.1.call-update
  7.9 0.0 all-gather.6.cloned.1.call-start
  8.0 25.4 %all-gather.4.cloned.1.call-done.s_ref = f32[1024,1024]{1,0:T(8,128)} async-done(((f32[512,1024]{1,0:T(8,128)}), f32[1024,1024]{1,0:T(8,128)}) %all-gather.4.cloned.1.call-update) | async-done | bytes 4194320 | tf_op jit(solution)/shard_map/all_gather | solution.py:247
  33.4 0.0 copy-start
  33.4 2.2 copy-done
  35.6 0.0 copy-start.1
  35.6 0.9 copy-done.1
  36.5 192.4 %shard_map.77 = (f32[32,1024]{1,0:T(8,128)}, bf16[8,32,128]{2,1,0:T(8,128)(2,1)}, f32[6,8,128,256]{3,2,1,0:T(8,128)}) custom-call(f32[1024,1024]{1,0:T(8,128)S(1)} %copy-done, f32[32,1024]{1,0:T(8,128)S(1)} %bitcast.7, f32[6,8,128,256]{3,2,1,0:T(8,128)} %blocks_ref.1), custom_call_target="tpu_custom_call" | custom-call | tf_op jit(solution)/shard_map/pallas_call | solution.py:136
  228.9 0.0 all-gather.6.cloned.1.call-update
  228.9 0.0 copy-done.4
  228.9 0.0 copy-done.3
  228.9 0.2 select_reduce_fusion.1.col_at
  229.1 0.0 copy-done.2
  229.1 0.3 select_reduce_fusion.row_at
  229.4 125.5 %all-gather.6.cloned.1.call-done = bf16[2048,32,128]{2,1,0:T(8,128)(2,1)} async-done(((bf16[8,32,128]{2,1,0:T(8,128)(2,1)}), bf16[2048,32,128]{2,1,0:T(8,128)(2,1)}) %all-gather.6.cloned.1.call-update) | async-done | bytes 16777232 | tf_op jit(solution)/shard_map/all_gather | solution.py:249
  354.9 15.6 %copy.13 = bf16[32,4,2,8,32,128]{5,4,1,0,2,3:T(8,128)(2,1)} copy(bf16[32,4,2,8,32,128]{5,4,3,2,1,0:T(8,128)(2,1)} %bitcast.9) | data formatting | bytes 33554432 | tf_op jit(solution)/shard_map/reshape | solution.py:251
  370.6 9.8 %shard_map.78 = f32[6,8,128,256]{3,2,1,0:T(8,128)} custom-call(s32[6]{0:T(128)S(1)} %select_reduce_fusion.1.col_at, s32[6,8]{1,0:T(8,128)S(1)} %select_reduce_fusion.row_at, s32[1]{0:T(128)} %bitcast.2.half, bf16[8,2,32,4,32,128]{5,4,3,2,1,0:T(8,128)(2,1)} %bitcast.8, f32[6,8,128,256]{3,2,1,0:T(8,128)} %get-tuple-element.7.blocks_ref), custom_call_target="tpu_custom_call", output_to_operand_aliasing={{}: (4, {})} | custom-call | tf_op jit(solution)/shard_map/pallas_call | solution.py:221
  (2 shorter events, 0.0 us)
Async XLA Ops:
  7.2 221.7 %copy-start.4 = (s32[6]{0:T(128)S(1)}, s32[6]{0:T(128)}, u32[]{:S(2)}) copy-start(s32[6]{0:T(128)} %param.9) | copy-start | bytes 76
  7.2 221.8 %copy-start.3 = (s32[32]{0:T(128)S(1)}, s32[32]{0:T(128)}, u32[]{:S(2)}) copy-start(s32[32]{0:T(128)} %param.8) | copy-start | bytes 388
  7.2 221.9 %copy-start.2 = (s32[6,8]{1,0:T(8,128)S(1)}, s32[6,8]{1,0:T(8,128)}, u32[]{:S(2)}) copy-start(s32[6,8]{1,0:T(8,128)} %param.10) | copy-start | bytes 580
  7.2 26.2 %all-gather.4.cloned.1.call-start = ((), (), s32[]{:S(2)}) async-start(), calls=%async_computation | async-start | bytes 6291456 | tf_op jit(solution)/shard_map/all_gather | solution.py:247
  7.9 347.0 %all-gather.6.cloned.1.call-start = ((), (), s32[]{:S(2)}) async-start(), calls=%async_computation.1 | async-start | bytes 16842752 | tf_op jit(solution)/shard_map/all_gather | solution.py:249
  33.4 2.2 copy-start
  35.6 0.9 copy-start.1
Sparse Core Ops, SparseCore 0:
  9.8 23.5 all-gather.3
  229.0 125.8 all-gather.5

commit v2 on v1

--- a/solution.py
+++ b/solution.py
@@ -10,6 +10,8 @@
 HIGH = lax.Precision.HIGHEST
 NB = 128
 F32 = jnp.float32
+MESH = pl.DeviceIdType.MESH
+PLACES = (4, 8, 4)
 
 
 def lane_spread(x, c):
@@ -91,19 +93,127 @@
     return jnp.concatenate(inverse, axis=0)
 
 
-def factor_kernel(s_ref, r_ref, blocks_ref, x_ref, g_ref, copy_ref, u_ref, t_ref, linv_ref, dg_ref, y_ref, sem):
+def spreading(g_ref, own_ref, send_sem, recv_sem, local_sem):
+    _, _, nx, nz, ny, rows, _ = g_ref.shape
+    blk, h = lax.axis_index("blk"), lax.axis_index("row")
+    x, z, y = blk // (nz * ny), (blk // ny) % nz, blk % ny
+    first, second = pl.ds(0, rows // 2), pl.ds(rows // 2, rows // 2)
+    every = slice(None)
+
+    def device(x, z, y, h):
+        return ((x * nz + z) * ny + y, h)
+
+    along_x = [device((x + k) % nx, z, y, h) for k in range(1, nx)]
+    along_z = [device(x, (z + k) % nz, y, h) for k in range(1, nz)]
+    along_y = [device(x, z, (y + k) % ny, h) for k in range(1, ny)]
+    other = device(x, z, y, 1 - h)
+
+    def copies(p, at, pieces):
+        return [
+            pltpu.make_async_remote_copy(
+                src_ref=src,
+                dst_ref=dst,
+                send_sem=send_sem.at[p, at + i],
+                recv_sem=recv_sem.at[p, at + i],
+                device_id=target,
+                device_id_type=MESH,
+            )
+            for i, (src, dst, target) in enumerate(pieces)
+        ]
+
+    def to_z(p):
+        return copies(p, 0, [(own_ref.at[p], g_ref.at[p, h, x, z, y], d) for d in along_z])
+
+    def to_plane(p):
+        a, b = g_ref.at[p, h, x, every, y, first], g_ref.at[p, h, x, every, y, second]
+        return copies(p, nz - 1, [(a, a, d) for d in along_y] + [(b, b, d) for d in along_x])
+
+    def to_rest(p):
+        a, b = g_ref.at[p, h, x, every, every, first], g_ref.at[p, h, every, every, y, second]
+        at = nz - 1 + nx - 1 + ny - 1
+        return copies(p, at, [(a, a, d) for d in along_x] + [(b, b, d) for d in along_y])
+
+    def to_core(p):
+        return copies(p, nz - 1 + 2 * (nx - 1 + ny - 1), [(g_ref.at[p, h], g_ref.at[p, h], other)])
+
+    def keep(p):
+        return pltpu.make_async_copy(own_ref.at[p], g_ref.at[p, h, x, z, y], local_sem.at[p])
+
+    return [to_z, to_plane, to_rest, to_core], keep, along_x + along_z + along_y + [other]
+
+
+def factor_kernel(
+    diag_ref, r_ref, x_ref, g_ref,
+    s_ref, u_ref, t_ref, linv_ref, dg_ref, y_ref, own_ref,
+    strip_send, strip_sem, send_sem, recv_sem, local_sem,
+):
     steps = s_ref.shape[0] // NB
-    copy = pltpu.make_async_copy(blocks_ref, copy_ref, sem)
-    copy.start()
+    half_steps = steps // 2
+    blk, h = lax.axis_index("blk"), lax.axis_index("row")
+    stages, keep, peers = spreading(g_ref, own_ref, send_sem, recv_sem, local_sem)
+
+    def strip(i):
+        return diag_ref.at[pl.ds(i * NB, NB)], s_ref.at[pl.ds(pl.multiple_of((half_steps * h + i) * NB, NB), NB)]
+
+    def strip_copy(i):
+        src, dst = strip(i)
+        return pltpu.make_async_copy(src, dst, strip_sem.at[half_steps * h + i])
+
+    def strip_sent(i):
+        src, dst = strip(i)
+        return pltpu.make_async_remote_copy(
+            src_ref=src,
+            dst_ref=dst,
+            send_sem=strip_send.at[i],
+            recv_sem=strip_sem.at[half_steps * h + i],
+            device_id=(blk, 1 - h),
+            device_id_type=MESH,
+        )
+
+    def strip_wait(q):
+        dst = s_ref.at[pl.ds(pl.multiple_of(q * NB, NB), NB)]
+        pltpu.make_async_copy(diag_ref.at[pl.ds(0, NB)], dst, strip_sem.at[q]).wait()
+
+    def finish(stage, p):
+        for copy in stages[stage](p):
+            copy.wait_recv()
+
+    def begin(stage, p):
+        for copy in stages[stage](p):
+            copy.start()
+
+    for i in range(half_steps):
+        strip_copy(i).start()
+    barrier = pltpu.get_barrier_semaphore()
+    for peer in peers:
+        pl.semaphore_signal(barrier, inc=1, device_id=peer, device_id_type=MESH)
     u_ref[...] = jnp.zeros_like(u_ref)
     x_ref[...] = jnp.zeros_like(x_ref)
     linv_ref[...] = jnp.zeros_like(linv_ref)
     t_ref[1] = jnp.zeros(t_ref.shape[1:], F32)
+    y_ref[...] = r_ref[:, 0:NB]
+    pl.semaphore_wait(barrier, len(peers))
+    for i in range(half_steps):
+        strip_sent(i).start()
+    strip_wait(0)
     t_ref[0] = s_ref[0:NB, :]
     dg_ref[...] = s_ref[0:NB, 0:NB]
-    y_ref[...] = r_ref[:, 0:NB]
 
     def step(p, carry):
+        @pl.when(p + 1 < steps)
+        def _():
+            strip_wait(p + 1)
+
+        @pl.when(p >= 3)
+        def _():
+            finish(2, p - 3)
+            begin(3, p - 3)
+
+        @pl.when(p >= 2)
+        def _():
+            finish(1, p - 2)
+            begin(2, p - 2)
+
         cur = lax.rem(p, 2)
         oth = 1 - cur
         here = pl.ds(pl.multiple_of(p * NB, NB), NB)
@@ -117,44 +227,92 @@
         linv = block_inverse([dg_ref[8 * k : 8 * k + 8, :] for k in range(NB // 8)])
         linv_ref[...] = linv
         t_ref[oth] = t_next
+
+        @pl.when(p >= 1)
+        def _():
+            finish(0, p - 1)
+            keep(p - 1).wait()
+            begin(1, p - 1)
+
+        x_here = mm(y_ref[...], linv, 1, 1)
+        x_ref[:, here] = x_here
+        own_ref[p] = x_here.astype(jnp.bfloat16)
+        keep(p).start()
+        begin(0, p)
         u_after = mm(linv, t_ref[cur, :, after], 1, 0)
         dg_ref[...] = t_ref[oth, :, after] - mm(u_after, u_after, 0, 0)
-        x_here = mm(y_ref[...], linv, 1, 1)
-        x_ref[:, here] = x_here
-        g_ref[p] = x_here.astype(jnp.bfloat16)
         y_ref[...] = y_next - mm(x_here, u_after, 1, 0)
         return carry
 
     lax.fori_loop(0, steps, step, 0)
-    copy.wait()
-
-
-def factor(diag, rows, blocks):
-    order = diag.shape[0]
+    last = steps - 1
+    finish(2, last - 2)
+    begin(3, last - 2)
+    finish(1, last - 1)
+    begin(2, last - 1)
+    finish(0, last)
+    keep(last).wait()
+    begin(1, last)
+    finish(1, last)
+    begin(2, last)
+    finish(2, last - 1)
+    begin(3, last - 1)
+    finish(2, last)
+    begin(3, last)
+
+    def end(p, carry):
+        finish(3, p)
+        for stage in stages:
+            for copy in stage(p):
+                copy.wait_send()
+        return carry
+
+    lax.fori_loop(0, steps, end, 0)
+    for i in range(half_steps):
+        strip_sent(i).wait_send()
+
+
+def factor(diag, rows, places):
+    order = diag.shape[1]
+    steps = order // NB
+    per = rows.shape[0]
+    nx, nz, ny = places
+    sends = nz - 1 + 2 * (nx - 1 + ny - 1) + 1
     vmem = pl.BlockSpec(memory_space=pltpu.VMEM)
     anywhere = pl.BlockSpec(memory_space=pl.ANY)
+    dma = pltpu.SemaphoreType.DMA
     return pl.pallas_call(
         factor_kernel,
         out_shape=(
             jax.ShapeDtypeStruct(rows.shape, F32),
-            jax.ShapeDtypeStruct((order // NB, rows.shape[0], NB), jnp.bfloat16),
-            jax.ShapeDtypeStruct(blocks.shape, F32),
+            jax.ShapeDtypeStruct((steps, 2, nx, nz, ny, per, NB), jnp.bfloat16),
         ),
-        in_specs=[vmem, vmem, anywhere],
-        out_specs=[vmem, vmem, anywhere],
+        in_specs=[anywhere, vmem],
+        out_specs=[vmem, anywhere],
         scratch_shapes=[
+            pltpu.VMEM((order, order), F32),
             pltpu.VMEM((order, order), F32),
             pltpu.VMEM((2, NB, order), F32),
             pltpu.VMEM((NB, NB), F32),
             pltpu.VMEM((NB, NB), F32),
-            pltpu.VMEM((rows.shape[0], NB), F32),
-            pltpu.SemaphoreType.DMA,
+            pltpu.VMEM((per, NB), F32),
+            pltpu.VMEM((steps, per, NB), jnp.bfloat16),
+            dma((steps // 2,)),
+            dma((steps,)),
+            dma((steps, sends)),
+            dma((steps, sends)),
+            dma((steps,)),
         ],
-        compiler_params=pltpu.CompilerParams(vmem_limit_bytes=48 << 20),
-    )(diag, rows, blocks)
-
-
-def update_kernel(col_at, row_at, half, g_ref, blocks_ref, out_ref, col_buf, row_buf, blk_buf, col_sem, row_sem, blk_sem):
+        compiler_params=pltpu.CompilerParams(
+            collective_id=0, has_side_effects=True, vmem_limit_bytes=48 << 20
+        ),
+    )(diag, rows)
+
+
+def update_kernel(
+    col_at, row_at, half, g_ref, blocks_ref, x_ref, out_ref, x_out,
+    col_buf, row_buf, blk_buf, x_buf, col_sem, row_sem, blk_sem, x_sem,
+):
     slots, stored = blocks_ref.shape[:2]
     chunks = g_ref.shape[0]
     size = blk_buf.shape[2]
@@ -168,11 +326,19 @@
         at = jnp.minimum(jnp.maximum(row_at[s, r], 0), last)
         return pltpu.make_async_copy(g_ref.at[:, mine, at], row_buf.at[s, r], row_sem.at[s, r])
 
-    def blk_in(s):
-        return pltpu.make_async_copy(blocks_ref.at[s], blk_buf.at[s], blk_sem.at[s])
+    def blk_keep(s):
+        return pltpu.make_async_copy(blocks_ref.at[s], out_ref.at[s], blk_sem.at[s])
 
     def blk_out(s):
         return pltpu.make_async_copy(blk_buf.at[s], out_ref.at[s], blk_sem.at[s])
+
+    x_in = pltpu.make_async_copy(x_ref, x_buf, x_sem.at[0])
+    x_back = pltpu.make_async_copy(x_buf, x_out, x_sem.at[1])
+    x_in.start()
+    for s in range(slots):
+        @pl.when(col_at[s] < 0)
+        def _():
+            blk_keep(s).start()
 
     for s in range(slots):
         @pl.when(col_at[s] >= 0)
@@ -180,15 +346,15 @@
             col_copy(s).start()
             for r in range(stored):
                 row_copy(s, r).start()
-            blk_in(s).start()
-
+
+    x_in.wait()
+    x_back.start()
     for s in range(slots):
         @pl.when(col_at[s] >= 0)
         def _():
             col_copy(s).wait()
             for r in range(stored):
                 row_copy(s, r).wait()
-            blk_in(s).wait()
 
             @pl.loop(0, stored)
             def _(r):
@@ -202,7 +368,7 @@
                         (((1,), (1,)), ((), ())),
                         preferred_element_type=F32,
                     )
-                kept = blk_buf[s, r]
+                kept = blocks_ref[s, r]
                 blk_buf[s, r] = jnp.where(row_at[s, r] >= 0, kept - total, kept)
 
             blk_out(s).start()
@@ -212,28 +378,35 @@
         def _():
             blk_out(s).wait()
 
-
-def update(g, blocks, col_at, row_at, half):
+        @pl.when(col_at[s] < 0)
+        def _():
+            blk_keep(s).wait()
+
+    x_back.wait()
+
+
+def update(g, blocks, x, col_at, row_at, half):
     slots, stored, size, width = blocks.shape
     chunks, _, _, parts, rows, _ = g.shape
     smem = pl.BlockSpec(memory_space=pltpu.SMEM)
     anywhere = pl.BlockSpec(memory_space=pl.ANY)
     return pl.pallas_call(
         update_kernel,
-        out_shape=jax.ShapeDtypeStruct(blocks.shape, F32),
-        in_specs=[smem, smem, smem, anywhere, anywhere],
-        out_specs=anywhere,
+        out_shape=(jax.ShapeDtypeStruct(blocks.shape, F32), jax.ShapeDtypeStruct(x.shape, F32)),
+        in_specs=[smem, smem, smem, anywhere, pl.BlockSpec(memory_space=pltpu.VMEM), anywhere],
+        out_specs=[anywhere, anywhere],
         scratch_shapes=[
             pltpu.VMEM((slots, chunks, 2, parts, rows, NB), jnp.bfloat16),
             pltpu.VMEM((slots, stored, chunks, parts, rows, NB), jnp.bfloat16),
             pltpu.VMEM((slots, stored, size, width), F32),
+            pltpu.VMEM(x.shape, F32),
             pltpu.SemaphoreType.DMA((slots,)),
             pltpu.SemaphoreType.DMA((slots, stored)),
             pltpu.SemaphoreType.DMA((slots,)),
+            pltpu.SemaphoreType.DMA((2,)),
         ],
-        input_output_aliases={4: 0},
-        compiler_params=pltpu.CompilerParams(vmem_limit_bytes=40 << 20),
-    )(col_at, row_at, half, g, blocks)
+        compiler_params=pltpu.CompilerParams(vmem_limit_bytes=50 << 20),
+    )(col_at, row_at, half, g, blocks, x)
 
 
 def places(ids, row_ids):
@@ -244,15 +417,13 @@
 
 def local(diag_block, panel_rows, row_ids, col_ids, block_rows, blocks):
     pieces = row_ids.shape[0]
-    diag = lax.all_gather(diag_block, "row", axis=0, tiled=True)
-    x, g, kept = factor(diag, panel_rows[0], blocks)
-    gathered = lax.all_gather(g, ("blk", "row"), axis=0, tiled=False)
-    chunks, rows = g.shape[:2]
-    gathered = gathered.reshape(pieces, -1, 2, chunks, rows, NB).transpose(3, 2, 0, 1, 4, 5)
     col_at = places(col_ids, row_ids)
     row_at = places(block_rows, row_ids)
     half = lax.axis_index("row").astype(jnp.int32)[None]
-    return x[None], update(gathered, kept, col_at, row_at, half)
+    x, g = factor(diag_block, panel_rows[0], PLACES)
+    g = g.reshape(g.shape[0], 2, pieces, -1, g.shape[5], NB)
+    new_blocks, x = update(g, blocks, x, col_at, row_at, half)
+    return x[None], new_blocks
 
 
 def solution(mesh):

time: 387 us -> 126 us (0.33)
  waiting for transfers between devices: 152 us -> 0 us
  Pallas kernels: 202 us -> 118 us
  local copies, waits for them, and re-layouts: 18.7 us -> 2.49 us
  between operations: 14.1 us -> 0.66 us
    all_gather x2 -> x0, waiting for transfers between devices: 151 us -> none  [the longest x1 126 us: local(): gathered = lax.all_gather(g, ('blk', 'row'), axis=0, tiled=False)]
    pallas_call x1, Pallas kernels: 192 us -> 112 us  [factor(): pl.pallas_call(factor_kernel, out_shape=(jax.ShapeDtypeStruct(rows.shape,...]
    reshape x1 -> x0, local copies, waits for them, and re-layouts: 15.6 us -> none  [local(): gathered.reshape(pieces, -1, 2, chunks, rows, NB)]
  transfers between devices with their start and end apart: 2 -> 0, of which waited for: 2 -> 0; matrix products, arithmetic and copies ran while one was open for 0% -> 0% of each run, Pallas kernels for 0% -> 0%
where the time goes in v2:
time: 126 us; the launch traced here: 125 us
  Pallas kernels  118 us (94%)
  other arithmetic  3.15 us (2%)
  local copies, waits for them, and re-layouts  2.49 us (2%)
    pallas_call x1, Pallas kernels, factor(): pl.pallas_call(factor_kernel, out_shape=(jax.ShapeDtypeStruct(rows.shape,...  112 us
    pallas_call x1, Pallas kernels, update(): pl.pallas_call(update_kernel, out_shape=(jax.ShapeDtypeStruct(blocks.shap...  6.35 us

profile of v2, /device:TPU:1, one launch (start us, length us, event | category | flops | bytes accessed | tf_op | source)
XLA Modules:
  0.0 124.6 jit_solution(11693920420403300698)
XLA Ops:
  0.6 0.7 broadcast_compare_fusion.1
  1.3 0.9 select_reduce_fusion.1.col_at
  2.2 0.7 broadcast_compare_fusion
  2.8 0.9 select_reduce_fusion.row_at
  3.8 0.0 copy-start
  3.8 1.6 %copy-done = f32[512,1024]{1,0:T(8,128)S(1)} copy-done((f32[512,1024]{1,0:T(8,128)S(1)}, f32[512,1024]{1,0:T(8,128)}, u32[]{:S(2)}) %copy-start) | copy-done | bytes 2097176
  5.4 0.0 copy-start.1
  5.4 0.9 copy-done.1
  6.3 111.9 %shard_map.77 = (f32[32,1024]{1,0:T(8,128)S(1)}, bf16[8,2,4,8,4,32,128]{6,5,4,3,2,1,0:T(8,128)(2,1)}) custom-call(f32[512,1024]{1,0:T(8,128)S(1)} %copy-done, f32[32,1024]{1,0:T(8,128)S(1)} %bitcast.4), custom_call_target="tpu_custom_call" | custom-call | tf_op jit(solution)/shard_map/pallas_call | solution.py:284
  118.2 6.4 %shard_map.78 = (f32[6,8,128,256]{3,2,1,0:T(8,128)}, f32[32,1024]{1,0:T(8,128)}) custom-call(s32[6]{0:T(128)S(1)} %select_reduce_fusion.1.col_at, s32[6,8]{1,0:T(8,128)S(1)} %select_reduce_fusion.row_at, s32[1]{0:T(128)} %bitcast.half, bf16[8,2,32,4,32,128]{5,4,3,2,1,0:T(8,128)(2,1)} %bitcast.5, f32[6,8,128,256]{3,2,1,0:T(8,128)} %blocks_ref.1, ...), custom_call_target="tpu_custom_call" | custom-call | tf_op jit(solution)/shard_map/pallas_call | solution.py:393
Async XLA Ops:
  3.8 1.6 %copy-start = (f32[512,1024]{1,0:T(8,128)S(1)}, f32[512,1024]{1,0:T(8,128)}, u32[]{:S(2)}) copy-start(f32[512,1024]{1,0:T(8,128)} %diag_ref.1) | copy-start | bytes 6291460
  5.4 0.9 copy-start.1

commit v3 on v2

--- a/solution.py
+++ b/solution.py
@@ -128,18 +128,33 @@
         a, b = g_ref.at[p, h, x, every, y, first], g_ref.at[p, h, x, every, y, second]
         return copies(p, nz - 1, [(a, a, d) for d in along_y] + [(b, b, d) for d in along_x])
 
-    def to_rest(p):
+    plane = nz - 1 + nx - 1 + ny - 1
+    right, left = (x + 1) % nx, (x + nx - 1) % nx
+    up, down = (y + 1) % ny, (y + ny - 1) % ny
+
+    def to_next(p):
         a, b = g_ref.at[p, h, x, every, every, first], g_ref.at[p, h, every, every, y, second]
-        at = nz - 1 + nx - 1 + ny - 1
-        return copies(p, at, [(a, a, d) for d in along_x] + [(b, b, d) for d in along_y])
+        return copies(p, plane, [
+            (a, a, device(right, z, y, h)), (a, a, device(left, z, y, h)),
+            (b, b, device(x, z, up, h)), (b, b, device(x, z, down, h)),
+        ])
+
+    def to_far(p):
+        low, high = pl.ds(0, nz // 2), pl.ds(nz // 2, nz // 2)
+        a, b = g_ref.at[p, h, left, low, every, first], g_ref.at[p, h, right, high, every, first]
+        c, d = g_ref.at[p, h, every, low, down, second], g_ref.at[p, h, every, high, up, second]
+        return copies(p, plane + 4, [
+            (a, a, device(right, z, y, h)), (b, b, device(left, z, y, h)),
+            (c, c, device(x, z, up, h)), (d, d, device(x, z, down, h)),
+        ])
 
     def to_core(p):
-        return copies(p, nz - 1 + 2 * (nx - 1 + ny - 1), [(g_ref.at[p, h], g_ref.at[p, h], other)])
+        return copies(p, plane + 8, [(g_ref.at[p, h], g_ref.at[p, h], other)])
 
     def keep(p):
         return pltpu.make_async_copy(own_ref.at[p], g_ref.at[p, h, x, z, y], local_sem.at[p])
 
-    return [to_z, to_plane, to_rest, to_core], keep, along_x + along_z + along_y + [other]
+    return [to_z, to_plane, to_next, to_far, to_core], keep, along_x + along_z + along_y + [other]
 
 
 def factor_kernel(
@@ -181,6 +196,12 @@
     def begin(stage, p):
         for copy in stages[stage](p):
             copy.start()
+
+    def advance(stage, p):
+        finish(stage - 1, p)
+        if stage == 1:
+            keep(p).wait()
+        begin(stage, p)
 
     for i in range(half_steps):
         strip_copy(i).start()
@@ -199,40 +220,29 @@
     t_ref[0] = s_ref[0:NB, :]
     dg_ref[...] = s_ref[0:NB, 0:NB]
 
-    def step(p, carry):
+    def step(p, carry, begin_at, end_at):
         @pl.when(p + 1 < steps)
         def _():
             strip_wait(p + 1)
 
-        @pl.when(p >= 3)
-        def _():
-            finish(2, p - 3)
-            begin(3, p - 3)
-
-        @pl.when(p >= 2)
-        def _():
-            finish(1, p - 2)
-            begin(2, p - 2)
-
         cur = lax.rem(p, 2)
         oth = 1 - cur
+        done, todo = slice(0, (end_at - 1) * NB), slice(begin_at * NB, steps * NB)
         here = pl.ds(pl.multiple_of(p * NB, NB), NB)
         before = pl.ds(pl.multiple_of(jnp.maximum(p - 1, 0) * NB, NB), NB)
         after = pl.ds(pl.multiple_of(jnp.minimum(p + 1, steps - 1) * NB, NB), NB)
-        u_prev = mm(linv_ref[...], t_ref[oth], 1, 0)
-        u_ref[before, :] = u_prev
-        t_ref[cur] = t_ref[cur] - mm(u_ref[before, here], u_prev, 0, 0)
-        t_next = s_ref[after, :] - mm(u_ref[:, after], u_ref[...], 0, 0)
-        y_next = r_ref[:, after] - mm(x_ref[...], u_ref[:, after], 1, 0)
+        u_prev = mm(linv_ref[...], t_ref[oth, :, todo], 1, 0)
+        u_ref[before, todo] = u_prev
+        t_ref[cur, :, todo] = t_ref[cur, :, todo] - mm(u_ref[before, here], u_prev, 0, 0)
+        t_next = s_ref[after, todo] - mm(u_ref[done, after], u_ref[done, todo], 0, 0)
+        y_next = r_ref[:, after] - mm(x_ref[:, done], u_ref[done, after], 1, 0)
         linv = block_inverse([dg_ref[8 * k : 8 * k + 8, :] for k in range(NB // 8)])
         linv_ref[...] = linv
-        t_ref[oth] = t_next
-
-        @pl.when(p >= 1)
-        def _():
-            finish(0, p - 1)
-            keep(p - 1).wait()
-            begin(1, p - 1)
+        t_ref[oth, :, todo] = t_next
+        for stage in range(len(stages) - 1, 0, -1):
+            @pl.when(p >= stage)
+            def _(stage=stage):
+                advance(stage, p - stage)
 
         x_here = mm(y_ref[...], linv, 1, 1)
         x_ref[:, here] = x_here
@@ -244,24 +254,14 @@
         y_ref[...] = y_next - mm(x_here, u_after, 1, 0)
         return carry
 
-    lax.fori_loop(0, steps, step, 0)
+    for at in range(0, steps, 2):
+        lax.fori_loop(at, at + 2, functools.partial(step, begin_at=at, end_at=at + 2), 0)
     last = steps - 1
-    finish(2, last - 2)
-    begin(3, last - 2)
-    finish(1, last - 1)
-    begin(2, last - 1)
-    finish(0, last)
-    keep(last).wait()
-    begin(1, last)
-    finish(1, last)
-    begin(2, last)
-    finish(2, last - 1)
-    begin(3, last - 1)
-    finish(2, last)
-    begin(3, last)
+    for stage, p in [(4, last - 3), (3, last - 2), (2, last - 1), (1, last), (4, last - 2), (3, last - 1), (2, last), (4, last - 1), (3, last), (4, last)]:
+        advance(stage, p)
 
     def end(p, carry):
-        finish(3, p)
+        finish(len(stages) - 1, p)
         for stage in stages:
             for copy in stage(p):
                 copy.wait_send()
@@ -277,7 +277,7 @@
     steps = order // NB
     per = rows.shape[0]
     nx, nz, ny = places
-    sends = nz - 1 + 2 * (nx - 1 + ny - 1) + 1
+    sends = nz - 1 + nx - 1 + ny - 1 + 9
     vmem = pl.BlockSpec(memory_space=pltpu.VMEM)
     anywhere = pl.BlockSpec(memory_space=pl.ANY)
     dma = pltpu.SemaphoreType.DMA
@@ -304,7 +304,7 @@
             dma((steps,)),
         ],
         compiler_params=pltpu.CompilerParams(
-            collective_id=0, has_side_effects=True, vmem_limit_bytes=48 << 20
+            collective_id=0, has_side_effects=True, vmem_limit_bytes=60 << 20
         ),
     )(diag, rows)
 
@@ -313,33 +313,25 @@
     col_at, row_at, half, g_ref, blocks_ref, x_ref, out_ref, x_out,
     col_buf, row_buf, blk_buf, x_buf, col_sem, row_sem, blk_sem, x_sem,
 ):
-    slots, stored = blocks_ref.shape[:2]
+    slots, stored, size, _ = blocks_ref.shape
     chunks = g_ref.shape[0]
-    size = blk_buf.shape[2]
     mine = half[0]
-    last = g_ref.shape[2] - 1
 
     def col_copy(s):
         return pltpu.make_async_copy(g_ref.at[:, :, jnp.maximum(col_at[s], 0)], col_buf.at[s], col_sem.at[s])
 
     def row_copy(s, r):
-        at = jnp.minimum(jnp.maximum(row_at[s, r], 0), last)
+        at = jnp.maximum(row_at[s, r], 0)
         return pltpu.make_async_copy(g_ref.at[:, mine, at], row_buf.at[s, r], row_sem.at[s, r])
 
-    def blk_keep(s):
-        return pltpu.make_async_copy(blocks_ref.at[s], out_ref.at[s], blk_sem.at[s])
+    def blk_in(s):
+        return pltpu.make_async_copy(blocks_ref.at[s], blk_buf.at[s], blk_sem.at[s])
 
     def blk_out(s):
         return pltpu.make_async_copy(blk_buf.at[s], out_ref.at[s], blk_sem.at[s])
 
     x_in = pltpu.make_async_copy(x_ref, x_buf, x_sem.at[0])
     x_back = pltpu.make_async_copy(x_buf, x_out, x_sem.at[1])
-    x_in.start()
-    for s in range(slots):
-        @pl.when(col_at[s] < 0)
-        def _():
-            blk_keep(s).start()
-
     for s in range(slots):
         @pl.when(col_at[s] >= 0)
         def _():
@@ -347,41 +339,45 @@
             for r in range(stored):
                 row_copy(s, r).start()
 
+    for s in range(slots):
+        blk_in(s).start()
+    x_in.start()
+
+    for s in range(slots):
+        @pl.when(col_at[s] < 0)
+        def _():
+            blk_in(s).wait()
+            blk_out(s).start()
+
     x_in.wait()
     x_back.start()
     for s in range(slots):
         @pl.when(col_at[s] >= 0)
         def _():
+            blk_in(s).wait()
             col_copy(s).wait()
             for r in range(stored):
                 row_copy(s, r).wait()
-
-            @pl.loop(0, stored)
-            def _(r):
+            right = [
+                jnp.concatenate([col_buf[s, p + q].reshape(2 * size, NB) for q in range(2)], axis=1)
+                for p in range(0, chunks, 2)
+            ]
+            for r in range(stored):
                 total = jnp.zeros((size, 2 * size), F32)
                 for p in range(0, chunks, 2):
                     left = [row_buf[s, r, p + q].reshape(size, NB) for q in range(2)]
-                    right = [col_buf[s, p + q].reshape(2 * size, NB) for q in range(2)]
                     total += lax.dot_general(
                         jnp.concatenate(left, axis=1),
-                        jnp.concatenate(right, axis=1),
+                        right[p // 2],
                         (((1,), (1,)), ((), ())),
                         preferred_element_type=F32,
                     )
-                kept = blocks_ref[s, r]
+                kept = blk_buf[s, r]
                 blk_buf[s, r] = jnp.where(row_at[s, r] >= 0, kept - total, kept)
-
             blk_out(s).start()
 
     for s in range(slots):
-        @pl.when(col_at[s] >= 0)
-        def _():
-            blk_out(s).wait()
-
-        @pl.when(col_at[s] < 0)
-        def _():
-            blk_keep(s).wait()
-
+        blk_out(s).wait()
     x_back.wait()
 
 
@@ -393,24 +389,24 @@
     return pl.pallas_call(
         update_kernel,
         out_shape=(jax.ShapeDtypeStruct(blocks.shape, F32), jax.ShapeDtypeStruct(x.shape, F32)),
-        in_specs=[smem, smem, smem, anywhere, pl.BlockSpec(memory_space=pltpu.VMEM), anywhere],
+        in_specs=[smem, smem, smem, anywhere, anywhere, anywhere],
         out_specs=[anywhere, anywhere],
         scratch_shapes=[
             pltpu.VMEM((slots, chunks, 2, parts, rows, NB), jnp.bfloat16),
             pltpu.VMEM((slots, stored, chunks, parts, rows, NB), jnp.bfloat16),
-            pltpu.VMEM((slots, stored, size, width), F32),
+            pltpu.VMEM(blocks.shape, F32),
             pltpu.VMEM(x.shape, F32),
             pltpu.SemaphoreType.DMA((slots,)),
             pltpu.SemaphoreType.DMA((slots, stored)),
             pltpu.SemaphoreType.DMA((slots,)),
             pltpu.SemaphoreType.DMA((2,)),
         ],
-        compiler_params=pltpu.CompilerParams(vmem_limit_bytes=50 << 20),
+        compiler_params=pltpu.CompilerParams(vmem_limit_bytes=60 << 20),
     )(col_at, row_at, half, g, blocks, x)
 
 
 def places(ids, row_ids):
-    match = (row_ids == ids[..., None]) & (ids[..., None] >= 0)
+    match = row_ids == ids[..., None]
     at = jnp.arange(row_ids.shape[0], dtype=jnp.int32)
     return jnp.max(jnp.where(match, at, -1), axis=-1)
 

time: 126 us -> 105 us (0.83); the launches traced: 125 us -> 105 us
  Pallas kernels: 118 us -> 101 us
  local copies, waits for them, and re-layouts: 2.49 us -> 0 us
    pallas_call x1, Pallas kernels: 112 us -> 94.6 us  [factor(): pl.pallas_call(factor_kernel, out_shape=(jax.ShapeDtypeStruct(rows.shape,...]
    unnamed x4 -> x0, local copies, waits for them, and re-layouts: 2.49 us -> none
    ge x2 -> x0, other arithmetic: 1.35 us -> none  [places(): match = (row_ids == ids[..., None]) & (ids[..., None] >= 0)]
where the time goes in v3:
time: 105 us
  Pallas kernels  101 us (96%)
  other arithmetic  2.86 us (3%)
    pallas_call x1, Pallas kernels, factor(): pl.pallas_call(factor_kernel, out_shape=(jax.ShapeDtypeStruct(rows.shape,...  94.6 us
    pallas_call x1, Pallas kernels, update(): pl.pallas_call(update_kernel, out_shape=(jax.ShapeDtypeStruct(blocks.shap...  6.81 us
    reduce_max x2, other arithmetic, places(): return jnp.max(jnp.where(match, at, -1), axis=-1)  2.86 us

profile of v3, /device:TPU:1, one launch (start us, length us, event | category | flops | bytes accessed | tf_op | source)
XLA Modules:
  0.0 105.1 jit_solution(16275945276228799739)
XLA Ops:
  0.6 1.3 %select_reduce_fusion.1.col_at = s32[6]{0:T(128)} fusion(s32[32]{0:T(128)} %param.8, s32[6]{0:T(128)} %param.9), kind=kLoop, calls=%fused_computation.1 | loop fusion | flops 570 | bytes 176 | tf_op jit(solution)/shard_map/reduce_max | solution.py:411
  2.0 1.5 %select_reduce_fusion.row_at = s32[6,8]{1,0:T(8,128)} fusion(s32[6,8]{1,0:T(8,128)} %param.10, s32[32]{0:T(128)} %param.8), kind=kLoop, calls=%fused_computation | loop fusion | flops 4560 | bytes 512 | tf_op jit(solution)/shard_map/reduce_max | solution.py:411
  3.5 94.6 %shard_map.77 = (f32[32,1024]{1,0:T(8,128)}, bf16[8,2,4,8,4,32,128]{6,5,4,3,2,1,0:T(8,128)(2,1)}) custom-call(f32[512,1024]{1,0:T(8,128)} %diag_ref.1, f32[32,1024]{1,0:T(8,128)} %bitcast.5), custom_call_target="tpu_custom_call" | custom-call | tf_op jit(solution)/shard_map/pallas_call | solution.py:284
  98.1 6.8 %shard_map.78 = (f32[6,8,128,256]{3,2,1,0:T(8,128)}, f32[32,1024]{1,0:T(8,128)}) custom-call(s32[6]{0:T(128)} %select_reduce_fusion.1.col_at, s32[6,8]{1,0:T(8,128)} %select_reduce_fusion.row_at, s32[1]{0:T(128)} %bitcast.half, bf16[8,2,32,4,32,128]{5,4,3,2,1,0:T(8,128)(2,1)} %bitcast.4, f32[6,8,128,256]{3,2,1,0:T(8,128)} %blocks_ref.1, ...), custom_call_target="tpu_custom_call" | custom-call | tf_op jit(solution)/shard_map/pallas_call | solution.py:389

commit v4 on v3

--- a/solution.py
+++ b/solution.py
@@ -11,6 +11,8 @@
 NB = 128
 F32 = jnp.float32
 MESH = pl.DeviceIdType.MESH
+LAGS = (0, 1, 2, 4, 5)
+POINTS = ("outer", "inner", "outer", "inner", "outer")
 PLACES = (4, 8, 4)
 
 
@@ -158,7 +160,7 @@
 
 
 def factor_kernel(
-    diag_ref, r_ref, x_ref, g_ref,
+    row_ids, col_ids, block_rows, diag_ref, r_ref, x_ref, g_ref, col_at, row_at,
     s_ref, u_ref, t_ref, linv_ref, dg_ref, y_ref, own_ref,
     strip_send, strip_sem, send_sem, recv_sem, local_sem,
 ):
@@ -213,6 +215,11 @@
     linv_ref[...] = jnp.zeros_like(linv_ref)
     t_ref[1] = jnp.zeros(t_ref.shape[1:], F32)
     y_ref[...] = r_ref[:, 0:NB]
+    for ids, at in ((col_ids, col_at), (block_rows, row_at)):
+        found = jnp.full(ids.shape, -1, jnp.int32)
+        for k in range(row_ids.shape[0]):
+            found = jnp.where(ids[...] == row_ids[k], k, found)
+        at[...] = found
     pl.semaphore_wait(barrier, len(peers))
     for i in range(half_steps):
         strip_sent(i).start()
@@ -239,11 +246,15 @@
         linv = block_inverse([dg_ref[8 * k : 8 * k + 8, :] for k in range(NB // 8)])
         linv_ref[...] = linv
         t_ref[oth, :, todo] = t_next
-        for stage in range(len(stages) - 1, 0, -1):
-            @pl.when(p >= stage)
-            def _(stage=stage):
-                advance(stage, p - stage)
-
+
+        def advance_due(point):
+            for stage in range(len(stages) - 1, 0, -1):
+                if POINTS[stage] == point:
+                    @pl.when(p >= LAGS[stage])
+                    def _(stage=stage):
+                        advance(stage, p - LAGS[stage])
+
+        advance_due("inner")
         x_here = mm(y_ref[...], linv, 1, 1)
         x_ref[:, here] = x_here
         own_ref[p] = x_here.astype(jnp.bfloat16)
@@ -252,13 +263,14 @@
         u_after = mm(linv, t_ref[cur, :, after], 1, 0)
         dg_ref[...] = t_ref[oth, :, after] - mm(u_after, u_after, 0, 0)
         y_ref[...] = y_next - mm(x_here, u_after, 1, 0)
+        advance_due("outer")
         return carry
 
     for at in range(0, steps, 2):
         lax.fori_loop(at, at + 2, functools.partial(step, begin_at=at, end_at=at + 2), 0)
-    last = steps - 1
-    for stage, p in [(4, last - 3), (3, last - 2), (2, last - 1), (1, last), (4, last - 2), (3, last - 1), (2, last), (4, last - 1), (3, last), (4, last)]:
-        advance(stage, p)
+    left = [(p + stage, -stage) for stage in range(1, len(stages)) for p in range(steps) if p + LAGS[stage] >= steps]
+    for when, stage in sorted(left):
+        advance(-stage, when + stage)
 
     def end(p, carry):
         finish(len(stages) - 1, p)
@@ -272,7 +284,7 @@
         strip_sent(i).wait_send()
 
 
-def factor(diag, rows, places):
+def factor(row_ids, col_ids, block_rows, diag, rows, places):
     order = diag.shape[1]
     steps = order // NB
     per = rows.shape[0]
@@ -286,9 +298,11 @@
         out_shape=(
             jax.ShapeDtypeStruct(rows.shape, F32),
             jax.ShapeDtypeStruct((steps, 2, nx, nz, ny, per, NB), jnp.bfloat16),
+            jax.ShapeDtypeStruct(col_ids.shape, jnp.int32),
+            jax.ShapeDtypeStruct(block_rows.shape, jnp.int32),
         ),
-        in_specs=[anywhere, vmem],
-        out_specs=[vmem, anywhere],
+        in_specs=[pl.BlockSpec(memory_space=pltpu.SMEM), vmem, vmem, anywhere, vmem],
+        out_specs=[vmem, anywhere, vmem, vmem],
         scratch_shapes=[
             pltpu.VMEM((order, order), F32),
             pltpu.VMEM((order, order), F32),
@@ -306,7 +320,7 @@
         compiler_params=pltpu.CompilerParams(
             collective_id=0, has_side_effects=True, vmem_limit_bytes=60 << 20
         ),
-    )(diag, rows)
+    )(row_ids, col_ids, block_rows, diag, rows)
 
 
 def update_kernel(
@@ -318,7 +332,7 @@
     mine = half[0]
 
     def col_copy(s):
-        return pltpu.make_async_copy(g_ref.at[:, :, jnp.maximum(col_at[s], 0)], col_buf.at[s], col_sem.at[s])
+        return pltpu.make_async_copy(g_ref.at[:, :, jnp.maximum(col_at[0, s], 0)], col_buf.at[s], col_sem.at[s])
 
     def row_copy(s, r):
         at = jnp.maximum(row_at[s, r], 0)
@@ -333,7 +347,7 @@
     x_in = pltpu.make_async_copy(x_ref, x_buf, x_sem.at[0])
     x_back = pltpu.make_async_copy(x_buf, x_out, x_sem.at[1])
     for s in range(slots):
-        @pl.when(col_at[s] >= 0)
+        @pl.when(col_at[0, s] >= 0)
         def _():
             col_copy(s).start()
             for r in range(stored):
@@ -344,7 +358,7 @@
     x_in.start()
 
     for s in range(slots):
-        @pl.when(col_at[s] < 0)
+        @pl.when(col_at[0, s] < 0)
         def _():
             blk_in(s).wait()
             blk_out(s).start()
@@ -352,7 +366,7 @@
     x_in.wait()
     x_back.start()
     for s in range(slots):
-        @pl.when(col_at[s] >= 0)
+        @pl.when(col_at[0, s] >= 0)
         def _():
             blk_in(s).wait()
             col_copy(s).wait()
@@ -405,18 +419,10 @@
     )(col_at, row_at, half, g, blocks, x)
 
 
-def places(ids, row_ids):
-    match = row_ids == ids[..., None]
-    at = jnp.arange(row_ids.shape[0], dtype=jnp.int32)
-    return jnp.max(jnp.where(match, at, -1), axis=-1)
-
-
 def local(diag_block, panel_rows, row_ids, col_ids, block_rows, blocks):
     pieces = row_ids.shape[0]
-    col_at = places(col_ids, row_ids)
-    row_at = places(block_rows, row_ids)
     half = lax.axis_index("row").astype(jnp.int32)[None]
-    x, g = factor(diag_block, panel_rows[0], PLACES)
+    x, g, col_at, row_at = factor(row_ids, col_ids[None], block_rows, diag_block, panel_rows[0], PLACES)
     g = g.reshape(g.shape[0], 2, pieces, -1, g.shape[5], NB)
     new_blocks, x = update(g, blocks, x, col_at, row_at, half)
     return x[None], new_blocks

time: 105 us -> 101 us (0.962)
  other arithmetic: 2.86 us -> 0 us
  Pallas kernels: 101 us -> 99.6 us
    pallas_call x1, Pallas kernels: 94.6 us -> 91.2 us  [factor(): pl.pallas_call(factor_kernel, out_shape=(jax.ShapeDtypeStruct(rows.shape,...]
    reduce_max x2 -> x0, other arithmetic: 2.86 us -> none  [places(): return jnp.max(jnp.where(match, at, -1), axis=-1)]
    pallas_call x1, Pallas kernels: 6.81 us -> 8.33 us  [update(): pl.pallas_call(update_kernel, out_shape=(jax.ShapeDtypeStruct(blocks.shap...]
where the time goes in v4:
time: 101 us; the launch traced here: 100 us
  Pallas kernels  99.6 us (99%)
    pallas_call x1, Pallas kernels, factor(): pl.pallas_call(factor_kernel, out_shape=(jax.ShapeDtypeStruct(rows.shape,...  91.2 us
    pallas_call x1, Pallas kernels, update(): pl.pallas_call(update_kernel, out_shape=(jax.ShapeDtypeStruct(blocks.shap...  8.33 us

profile of v4, /device:TPU:1, one launch (start us, length us, event | category | flops | bytes accessed | tf_op | source)
XLA Modules:
  0.0 100.4 jit_solution(7894291137963306068)
XLA Ops:
  0.6 91.2 %shard_map.77 = (f32[32,1024]{1,0:T(8,128)}, bf16[8,2,4,8,4,32,128]{6,5,4,3,2,1,0:T(8,128)(2,1)}, s32[1,6]{1,0:T(1,128)}, s32[6,8]{1,0:T(8,128)}) custom-call(s32[32]{0:T(128)} %row_ids.1, s32[1,6]{1,0:T(1,128)} %bitcast.7, s32[6,8]{1,0:T(8,128)} %block_rows.1, f32[512,1024]{1,0:T(8,128)} %diag_ref.1, f32[32,1024]{1,0:T(8,128)} %bitcast.6), custom_call_target="tpu_custom_call" | custom-call | tf_op jit(solution)/shard_map/pallas_call | solution.py:296
  91.9 8.3 %shard_map.78 = (f32[6,8,128,256]{3,2,1,0:T(8,128)}, f32[32,1024]{1,0:T(8,128)}) custom-call(s32[1,6]{1,0:T(1,128)} %get-tuple-element.8.col_at, s32[6,8]{1,0:T(8,128)} %get-tuple-element.9.row_at, s32[1]{0:T(128)} %bitcast.2.half, bf16[8,2,32,4,32,128]{5,4,3,2,1,0:T(8,128)(2,1)} %bitcast.5, f32[6,8,128,256]{3,2,1,0:T(8,128)} %blocks_ref.1, ...), custom_call_target="tpu_custom_call" | custom-call | tf_op jit(solution)/shard_map/pallas_call | solution.py:403

commit v5 on v4

--- a/solution.py
+++ b/solution.py
@@ -268,9 +268,9 @@
 
     for at in range(0, steps, 2):
         lax.fori_loop(at, at + 2, functools.partial(step, begin_at=at, end_at=at + 2), 0)
-    left = [(p + stage, -stage) for stage in range(1, len(stages)) for p in range(steps) if p + LAGS[stage] >= steps]
-    for when, stage in sorted(left):
-        advance(-stage, when + stage)
+    left = [(stage, p) for stage in range(1, len(stages)) for p in range(steps) if p + LAGS[stage] >= steps]
+    for stage, p in sorted(left, key=lambda due: (due[1] + 2 * due[0], -due[0])):
+        advance(stage, p)
 
     def end(p, carry):
         finish(len(stages) - 1, p)
@@ -346,22 +346,19 @@
 
     x_in = pltpu.make_async_copy(x_ref, x_buf, x_sem.at[0])
     x_back = pltpu.make_async_copy(x_buf, x_out, x_sem.at[1])
+    x_in.start()
     for s in range(slots):
         @pl.when(col_at[0, s] >= 0)
         def _():
             col_copy(s).start()
             for r in range(stored):
                 row_copy(s, r).start()
-
-    for s in range(slots):
-        blk_in(s).start()
-    x_in.start()
+            blk_in(s).start()
 
     for s in range(slots):
         @pl.when(col_at[0, s] < 0)
         def _():
-            blk_in(s).wait()
-            blk_out(s).start()
+            blk_in(s).start()
 
     x_in.wait()
     x_back.start()
@@ -391,6 +388,12 @@
             blk_out(s).start()
 
     for s in range(slots):
+        @pl.when(col_at[0, s] < 0)
+        def _():
+            blk_in(s).wait()
+            blk_out(s).start()
+
+    for s in range(slots):
         blk_out(s).wait()
     x_back.wait()
 

time: 101 us -> 93.4 us (0.925)
  Pallas kernels: 99.6 us -> 91.2 us
    pallas_call x1, Pallas kernels: 91.2 us -> 84.6 us  [factor(): pl.pallas_call(factor_kernel, out_shape=(jax.ShapeDtypeStruct(rows.shape,...]
    pallas_call x1, Pallas kernels: 8.33 us -> 6.64 us  [update(): pl.pallas_call(update_kernel, out_shape=(jax.ShapeDtypeStruct(blocks.shap...]
where the time goes in v5:
time: 93.4 us; the launch traced here: 92 us
  Pallas kernels  91.2 us (98%)
    pallas_call x1, Pallas kernels, factor(): pl.pallas_call(factor_kernel, out_shape=(jax.ShapeDtypeStruct(rows.shape,...  84.6 us
    pallas_call x1, Pallas kernels, update(): pl.pallas_call(update_kernel, out_shape=(jax.ShapeDtypeStruct(blocks.shap...  6.64 us

profile of v5, /device:TPU:1, one launch (start us, length us, event | category | flops | bytes accessed | tf_op | source)
XLA Modules:
  0.0 92.0 jit_solution(13337714100274712814)
XLA Ops:
  0.6 84.6 %shard_map.77 = (f32[32,1024]{1,0:T(8,128)}, bf16[8,2,4,8,4,32,128]{6,5,4,3,2,1,0:T(8,128)(2,1)}, s32[1,6]{1,0:T(1,128)}, s32[6,8]{1,0:T(8,128)}) custom-call(s32[32]{0:T(128)} %row_ids.1, s32[1,6]{1,0:T(1,128)} %bitcast.7, s32[6,8]{1,0:T(8,128)} %block_rows.1, f32[512,1024]{1,0:T(8,128)} %diag_ref.1, f32[32,1024]{1,0:T(8,128)} %bitcast.6), custom_call_target="tpu_custom_call" | custom-call | tf_op jit(solution)/shard_map/pallas_call | solution.py:296
  85.2 6.6 %shard_map.78 = (f32[6,8,128,256]{3,2,1,0:T(8,128)}, f32[32,1024]{1,0:T(8,128)}) custom-call(s32[1,6]{1,0:T(1,128)} %get-tuple-element.8.col_at, s32[6,8]{1,0:T(8,128)} %get-tuple-element.9.row_at, s32[1]{0:T(128)} %bitcast.2.half, bf16[8,2,32,4,32,128]{5,4,3,2,1,0:T(8,128)(2,1)} %bitcast.5, f32[6,8,128,256]{3,2,1,0:T(8,128)} %blocks_ref.1, ...), custom_call_target="tpu_custom_call" | custom-call | tf_op jit(solution)/shard_map/pallas_call | solution.py:406
